TPU v7x, 32 devices: a whole 2x2x4 slice. The times are simulated.
32 devices in a mesh: dp: 8 (over y, x, core), chan: 4 (over z).
Axes of the slice: x: 2, y: 2, z: 4, core: 2. Of those that a mesh axis runs over, the one named last changes fastest.
Arguments:
- signal: bfloat16 [8, 512, 8192], P('dp', 'chan'), may hold values from -6 to 6
- signal_grad: bfloat16 [8, 512, 8192], P('dp', 'chan'), may hold values from -6 to 6
- embed_weight: float32 [64, 33], replicated, may hold values from -1 to 1
- embed_bias: float32 [64], replicated, may hold values from -3.140625 to 3.140625
- hidden_weight: float32 [64, 64], replicated, may hold values from -0.75 to 0.75
- frequency: float32 [2, 64], replicated, may hold values from 0.5 to 2
- output_weight: float32 [512, 64], replicated, may hold values from -0.75 to 0.75
- decay_rate: float32 [512], replicated, may hold values from 0.3 to 30
Outputs:
- filter_grad: float32 [512, 16384], P(None, ('dp', 'chan'))
- embed_grad: float32 [64, 33], replicated
- bias_grad: float32 [64], replicated
- hidden_grad: float32 [64, 64], replicated
- frequency_grad: float32 [2, 64], replicated
- output_grad: float32 [512, 64], replicated
- decay_grad: float32 [512], replicated
All inputs are finite; a program needn't handle non-finite values.
Results may differ from a plain program's by a relative error of at most 0.0003.
Values may be sent and summed in bfloat16 or wider, within the bound.
No kernel may reach another device: no remote copies, remote signals or barrier semaphores. Data moves between devices by JAX's collectives and lax.ppermute only.
A program may use at most 64 MiB of HBM per device.

v0:
```python
import math
import jax
import jax.numpy as jnp
from jax import lax
from jax.sharding import PartitionSpec as P


def lag_features(lag, length, bands):
    total = 2 * length
    scaled = lag.astype(jnp.float32) / length
    sines = []
    cosines = []
    for band in range(bands):
        factor = max(1, int(0.45 * total * 10000.0 ** (-band / bands)))
        phase = (lag * factor % total).astype(jnp.float32) * (2.0 * math.pi / total)
        sines.append(jnp.sin(phase))
        cosines.append(jnp.cos(phase))
    return jnp.stack([scaled] + sines + cosines)


def filter_loss(params, lag, cotangent, length):
    embed_weight, embed_bias, hidden_weight, frequency, output_weight, decay_rate = params
    bands = (embed_weight.shape[1] - 1) // 2
    exact = lax.Precision.HIGHEST
    table = lag_features(lag, length, bands)
    first = jnp.sin(
        frequency[0][:, None]
        * (
            jnp.dot(embed_weight, table, precision=exact, preferred_element_type=jnp.float32)
            + embed_bias[:, None]
        )
    )
    second = jnp.sin(
        frequency[1][:, None]
        * jnp.dot(hidden_weight, first, precision=exact, preferred_element_type=jnp.float32)
    )
    shaped = jnp.dot(output_weight, second, precision=exact, preferred_element_type=jnp.float32)
    window = jnp.exp(-decay_rate[:, None] * jnp.abs(lag).astype(jnp.float32)[None, :] / length)
    return jnp.sum(shaped * window * cotangent) / math.sqrt(2 * length)


def plan_sizes(total):
    bits = total.bit_length() - 1
    side = 2 ** min(7, bits // 2)
    return (total // (side * side), side, side)


def rotation(rows, cols, modulus, sign):
    row_index = jnp.arange(rows, dtype=jnp.int32)
    col_index = jnp.arange(cols, dtype=jnp.int32)
    product = row_index[:, None] * col_index[None, :] % modulus
    angle = product.astype(jnp.float32) * (-2.0 * math.pi / modulus)
    return (jnp.cos(angle), sign * jnp.sin(angle))


def twist(real_part, imag_part, table):
    cosine, sine = table
    return (real_part * cosine - imag_part * sine, real_part * sine + imag_part * cosine)


def table_product(spec, table, real_part, imag_part, table_first):
    cosine, sine = table
    exact = lax.Precision.HIGHEST

    def apply(matrix, values):
        if table_first:
            return jnp.einsum(
                spec, matrix, values, precision=exact, preferred_element_type=jnp.float32
            )
        return jnp.einsum(spec, values, matrix, precision=exact, preferred_element_type=jnp.float32)

    common = apply(cosine, real_part + imag_part)
    return (common - apply(cosine + sine, imag_part), common + apply(sine - cosine, real_part))


def forward(real_part, imag_part, total):
    outer, middle, inner = plan_sizes(total)
    leading = real_part.shape[:-1]
    real_part = real_part.reshape(leading + (outer, middle * inner))
    imag_part = imag_part.reshape(leading + (outer, middle * inner))
    real_part, imag_part = table_product(
        "kp,...pm->...km", rotation(outer, outer, outer, 1.0), real_part, imag_part, True
    )
    real_part, imag_part = twist(real_part, imag_part, rotation(outer, middle * inner, total, 1.0))
    real_part = real_part.reshape(leading + (outer, middle, inner))
    imag_part = imag_part.reshape(leading + (outer, middle, inner))
    real_part, imag_part = table_product(
        "aq,...kqr->...kar", rotation(middle, middle, middle, 1.0), real_part, imag_part, True
    )
    real_part, imag_part = twist(real_part, imag_part, rotation(middle, inner, middle * inner, 1.0))
    return table_product(
        "...kar,rb->...kab", rotation(inner, inner, inner, 1.0), real_part, imag_part, False
    )


def inverse(real_part, imag_part, total):
    outer, middle, inner = plan_sizes(total)
    leading = real_part.shape[:-3]
    exact = lax.Precision.HIGHEST
    real_part, imag_part = table_product(
        "...kab,rb->...kar", rotation(inner, inner, inner, -1.0), real_part, imag_part, False
    )
    real_part, imag_part = twist(
        real_part, imag_part, rotation(middle, inner, middle * inner, -1.0)
    )
    real_part, imag_part = table_product(
        "qa,...kar->...kqr", rotation(middle, middle, middle, -1.0), real_part, imag_part, True
    )
    real_part = real_part.reshape(leading + (outer, middle * inner))
    imag_part = imag_part.reshape(leading + (outer, middle * inner))
    real_part, imag_part = twist(real_part, imag_part, rotation(outer, middle * inner, total, -1.0))
    cosine, sine = rotation(outer, outer, outer, -1.0)
    result = jnp.einsum(
        "pk,...km->...pm", cosine, real_part, precision=exact, preferred_element_type=jnp.float32
    )
    result = result - jnp.einsum(
        "pk,...km->...pm", sine, imag_part, precision=exact, preferred_element_type=jnp.float32
    )
    return result.reshape(leading + (total,)) / total


def mirror(values):
    flipped = jnp.flip(values, (-3, -2, -1))
    shifted = jnp.roll(flipped, 1, axis=-3)
    head = jnp.roll(shifted[..., 0, :, :], 1, axis=-2)
    first_row = (jnp.arange(head.shape[-2]) == 0)[:, None]
    head = jnp.where(first_row, jnp.roll(head, 1, axis=-1), head)
    return jnp.concatenate([head[..., None, :, :], shifted[..., 1:, :, :]], axis=-3)


def block_spectrum(inputs, grads, total):
    padding = jnp.zeros(inputs.shape[:-1] + (total - inputs.shape[-1],), jnp.float32)
    real_part = jnp.concatenate([inputs.astype(jnp.float32), padding], axis=-1)
    imag_part = jnp.concatenate([grads.astype(jnp.float32), padding], axis=-1)
    spectrum_real, spectrum_imag = forward(real_part, imag_part, total)
    back_real = mirror(spectrum_real)
    back_imag = -mirror(spectrum_imag)
    in_real = 0.5 * (spectrum_real + back_real)
    in_imag = 0.5 * (spectrum_imag + back_imag)
    grad_real = 0.5 * (spectrum_imag - back_imag)
    grad_imag = -0.5 * (spectrum_real - back_real)
    cross_real = in_real * grad_real + in_imag * grad_imag
    cross_imag = in_real * grad_imag - in_imag * grad_real
    return (jnp.sum(cross_real, axis=0), jnp.sum(cross_imag, axis=0))


def local(
    signal,
    signal_grad,
    embed_weight,
    embed_bias,
    hidden_weight,
    frequency,
    output_weight,
    decay_rate,
):
    seq_local, chan_local, length = signal.shape
    total = 2 * length
    block = 8
    scale = 1.0 / math.sqrt(seq_local * lax.axis_size("dp") * length)
    indices = jnp.arange(chan_local // block, dtype=jnp.int32)

    def spectrum_of(index):
        start = index * block
        inputs = lax.dynamic_slice_in_dim(signal, start, block, 1)
        grads = lax.dynamic_slice_in_dim(signal_grad, start, block, 1)
        return block_spectrum(inputs, grads, total)

    def lags_of(index):
        cross_real, cross_imag = spectrum_of(index)
        return inverse(cross_real, cross_imag, total)

    correlation = lax.map(lags_of, indices).reshape(chan_local, total) * scale
    shared = lax.psum_scatter(correlation, "dp", scatter_dimension=1, tiled=True)
    filter_grad = lax.all_to_all(shared, "chan", split_axis=1, concat_axis=0, tiled=True)
    lag_count = filter_grad.shape[1]
    device_rank = lax.axis_index("dp") * lax.axis_size("chan") + lax.axis_index("chan")
    position = device_rank * lag_count + jnp.arange(lag_count, dtype=jnp.int32)
    lag = jnp.where(position < length, position, position - total)
    params = (embed_weight, embed_bias, hidden_weight, frequency, output_weight, decay_rate)
    local_grads = jax.grad(filter_loss)(params, lag, filter_grad, length)
    summed = lax.psum(
        (
            local_grads[0],
            local_grads[1],
            local_grads[2],
            local_grads[3],
            local_grads[4],
            local_grads[5],
        ),
        ("dp", "chan"),
    )
    return (filter_grad, summed[0], summed[1], summed[2], summed[3], summed[4], summed[5])


def solution(mesh):
    placed = (P("dp", "chan", None), P("dp", "chan", None), P(), P(), P(), P(), P(), P())
    return jax.shard_map(
        local,
        mesh=mesh,
        in_specs=placed,
        out_specs=(P(None, ("dp", "chan")), P(), P(), P(), P(), P(), P()),
        check_vma=False,
    )
```

profile of v0, /device:TPU:0, one launch (start us, length us, event | category | flops | bytes accessed | tf_op | source)
XLA Modules:
  0.0 587.0 jit_solution(18230572061578156664)
XLA Ops:
  7.2 325.0 %while.13 = (s32[]{:T(128)}, f32[16,8,16384]{2,1,0:T(8,128)}, s32[16]{0:T(128)S(1)}, bf16[1,128,8192]{2,1,0:T(8,128)(2,1)}, bf16[1,128,8192]{2,1,0:T(8,128)(2,1)...) while((s32[]{:T(128)}, f32[16,8,16384]{2,1,0:T(8,128)}, s32[16]{0:T(128)S(1)}, ...), condition=%wide.region_1.2_spmd, body=%wide.region_0.1_spmd.sunk | while | flops 2430353408 | bytes 44499364 | solution.py:173
  13.4 1.3 fusion.309
  33.7 1.3 fusion.309
  54.0 1.3 fusion.309
  74.4 1.3 fusion.309
  94.7 1.3 fusion.309
  115.0 1.3 fusion.309
  135.3 1.3 fusion.309
  155.6 1.3 fusion.309
  175.9 1.3 fusion.309
  196.3 1.3 fusion.309
  216.6 1.3 fusion.309
  332.3 7.4 %multiply_bitcast_fusion = f32[128,16384]{1,0:T(8,128)} fusion(f32[16,8,16384]{2,1,0:T(8,128)} %get-tuple-element.175), kind=kLoop, calls=%fused_computation.149 | loop fusion | flops 2097152 | bytes 16777216 | tf_op jit(solution)/shard_map/mul | solution.py:173
  342.0 72.2 %reduce-scatter.2.cloned.1.call-done = f32[128,2048]{1,0:T(8,128)} async-done(((f32[128,16384]{1,0:T(8,128)}), f32[128,2048]{1,0:T(8,128)}) %reduce-scatter.2.cloned.1.call-update) | async-done | bytes 1048592 | tf_op jit(solution)/shard_map/reduce_scatter | solution.py:174
  414.1 2.5 copy.73
  416.7 4.6 all-to-all-start
  423.4 23.4 %all-to-all-done = f32[128,4,512]{0,2,1:T(8,128)S(1)} async-done(((f32[128,4,512]{0,2,1:T(8,128)}), f32[128,4,512]{0,2,1:T(8,128)S(1)}, u32[]{:S(2)}, u32[]{:S(2)}) %all-to-all-start) | async-done | bytes 1048608 | tf_op jit(solution)/shard_map/all_to_all | solution.py:175
  446.8 1.8 multiply_reduce_fusion.1
  450.4 1.3 copy.75
  452.0 1.7 fusion.113
  453.7 2.2 fusion.118
  455.9 38.1 %all-reduce.4 = (f32[64,33]{0,1:T(8,128)}, f32[64]{0:T(128)}, f32[64,64]{1,0:T(8,128)}, f32[2,64]{1,0:T(2,128)}, f32[512]{0:T(512)}) all-reduce(f32[64,33]{0,1:T(8,128)S(1)} %fusion.129, f32[64]{0:T(128)S(1)} %get-tuple-element.198, f32[64,64]{1,0:T(8,128)S(1)} %fusion.131, ...), channel_id=1, replica_groups=mesh['dp'=8,'chan'=4] {'dp','chan'}, use_global_device_ids=true, to_apply=%region_3.4 | all-reduce | flops 6912 | bytes 55296 | tf_op jit(solution)/shard_map/psum | solution.py:182
  494.0 84.7 %all-reduce.7.cloned.1.call-done = f32[512,64]{0,1:T(8,128)} async-done(((f32[512,64]{0,1:T(8,128)}), f32[512,64]{0,1:T(8,128)}) %all-reduce.7.cloned.1.call-update) | async-done | bytes 131088 | tf_op jit(solution)/shard_map/psum | solution.py:182
  578.6 1.6 copy.124
  (613 shorter events, 303.4 us)
Async XLA Ops:
  7.2 439.7 %copy-start = (f32[512,64]{0,1:T(8,128)S(1)}, f32[512,64]{0,1:T(8,128)}, u32[]{:S(2)}) copy-start(f32[512,64]{0,1:T(8,128)} %param.16) | copy-start | bytes 393220
  7.2 407.0 %reduce-scatter.2.cloned.1.call-start = ((), (), s32[]{:S(2)}) async-start(), calls=%async_computation.2 | async-start | bytes 9437184 | tf_op jit(solution)/shard_map/reduce_scatter | solution.py:174
  339.7 0.7 copy-start.3
  339.7 82.6 %copy-start.4 = (f32[2,64]{1,0:T(2,128)S(1)}, f32[2,64]{1,0:T(2,128)}, u32[]{:S(2)}) copy-start(f32[2,64]{1,0:T(2,128)} %param.15) | copy-start | bytes 1540
  339.7 82.6 %copy-start.2 = (f32[64,33]{0,1:T(8,128)S(1)}, f32[64,33]{0,1:T(8,128)}, u32[]{:S(2)}) copy-start(f32[64,33]{0,1:T(8,128)} %param.12) | copy-start | bytes 25348
  339.7 82.6 %copy-start.5 = (f32[64]{0:T(128)S(1)}, f32[64]{0:T(128)}, u32[]{:S(2)}) copy-start(f32[64]{0:T(128)} %param.13) | copy-start | bytes 772
  339.7 82.9 %copy-start.1 = (f32[64,64]{1,0:T(8,128)S(1)}, f32[64,64]{1,0:T(8,128)}, u32[]{:S(2)}) copy-start(f32[64,64]{1,0:T(8,128)} %param.14) | copy-start | bytes 49156
  416.7 30.2 %all-to-all-start = ((f32[128,4,512]{0,2,1:T(8,128)}), f32[128,4,512]{0,2,1:T(8,128)S(1)}, u32[]{:S(2)}, u32[]{:S(2)}) async-start(f32[128,4,512]{0,2,1:T(8,128)} %bitcast.39), calls=%async_computation.1 | async-start | bytes 2097152 | tf_op jit(solution)/shard_map/all_to_all | solution.py:175
  421.3 157.4 %all-reduce.7.cloned.1.call-start = ((), (), s32[]{:S(2)}) async-start(), calls=%async_computation.3 | async-start | bytes 262144 | tf_op jit(solution)/shard_map/psum | solution.py:182
Sparse Core Ops, SparseCore 0:
  339.9 74.2 reduce-scatter.1
  456.0 122.5 all-reduce.6
where the time goes:
time: 588 us; the launch traced here: 587 us
  matrix products  207 us (35%)
  waiting for transfers between devices  180 us (31%)
  local copies, waits for them, and re-layouts  88.7 us (15%)
  other arithmetic  40.2 us (7%)
  blocking collectives  38.1 us (6%)
  between operations  14.2 us (2%)
  loops' own time  14 us (2%)
    dot_general x96, matrix products, apply(): jnp.einsum(spec, values, matrix, precision=exact, preferred_element_type=...  99.2 us
    dot_general x96, matrix products, apply(): jnp.einsum(spec, matrix, values, precision=exact, preferred_element_type=...  99.1 us
    psum x1, waiting for transfers between devices, local(): lax.psum((local_grads[0], local_grads[1], local_grads[2], local_grads[3],...  84.7 us
    reduce_scatter x1, waiting for transfers between devices, local(): lax.psum_scatter(correlation, 'dp', scatter_dimension=1, tiled=True)  72.2 us
    psum x1, blocking collectives, local(): lax.psum((local_grads[0], local_grads[1], local_grads[2], local_grads[3],...  38.1 us
    all_to_all x1, waiting for transfers between devices, local(): lax.all_to_all(shared, 'chan', split_axis=1, concat_axis=0, tiled=True)  23.4 us
    another operation x32, local copies, waits for them, and re-layouts  22.9 us
    dynamic_update_slice x16, local copies, waits for them, and re-layouts, local(): correlation = lax.map(lags_of, indices).reshape(chan_local, total) * scale  18 us
  transfers between devices with their start and end apart: 3, of which 3 were waited for; matrix products, arithmetic and copies ran while one was open for 1% of the time, Pallas kernels for 0%

commit v1 on v0

--- a/solution.py
+++ b/solution.py
@@ -179,7 +179,7 @@
     lag = jnp.where(position < length, position, position - total)
     params = (embed_weight, embed_bias, hidden_weight, frequency, output_weight, decay_rate)
     local_grads = jax.grad(filter_loss)(params, lag, filter_grad, length)
-    summed = lax.psum(
+    half = lax.psum(
         (
             local_grads[0],
             local_grads[1],
@@ -188,8 +188,9 @@
             local_grads[4],
             local_grads[5],
         ),
-        ("dp", "chan"),
-    )
+        "chan",
+    )
+    summed = lax.psum(half, "dp")
     return (filter_grad, summed[0], summed[1], summed[2], summed[3], summed[4], summed[5])
 
 

time: 588 us -> 551 us (0.937)
  waiting for transfers between devices: 180 us -> 140 us
    psum x1, waiting for transfers between devices: 84.7 us -> 31 us  [local(): lax.psum((local_grads[0], local_grads[1], local_grads[2], local_grads[3],...]
    psum x0 -> x1, blocking collectives: none -> 23.4 us  [local(): summed = lax.psum(half, 'dp')]
    psum x1, blocking collectives: 38.1 us -> 18.4 us  [local(): lax.psum((local_grads[0], local_grads[1], local_grads[2], local_grads[3],...]
    psum x0 -> x1, waiting for transfers between devices: none -> 13 us  [local(): summed = lax.psum(half, 'dp')]
  transfers between devices with their start and end apart: 3 -> 4, of which waited for: 3 -> 4; matrix products, arithmetic and copies ran while one was open for 1% -> 1% of each run, Pallas kernels for 0% -> 0%
where the time goes in v1:
time: 551 us; the launch traced here: 550 us
  matrix products  207 us (38%)
  waiting for transfers between devices  140 us (25%)
  local copies, waits for them, and re-layouts  88.7 us (16%)
  blocking collectives  41.8 us (8%)
  other arithmetic  40.2 us (7%)
  loops' own time  14 us (3%)
  between operations  13.9 us (3%)
    dot_general x96, matrix products, apply(): jnp.einsum(spec, values, matrix, precision=exact, preferred_element_type=...  99.2 us
    dot_general x96, matrix products, apply(): jnp.einsum(spec, matrix, values, precision=exact, preferred_element_type=...  99.1 us
    reduce_scatter x1, waiting for transfers between devices, local(): lax.psum_scatter(correlation, 'dp', scatter_dimension=1, tiled=True)  72.2 us
    psum x1, waiting for transfers between devices, local(): lax.psum((local_grads[0], local_grads[1], local_grads[2], local_grads[3],...  31 us
    all_to_all x1, waiting for transfers between devices, local(): lax.all_to_all(shared, 'chan', split_axis=1, concat_axis=0, tiled=True)  23.4 us
    psum x1, blocking collectives, local(): summed = lax.psum(half, 'dp')  23.4 us
    another operation x32, local copies, waits for them, and re-layouts  22.9 us
    psum x1, blocking collectives, local(): lax.psum((local_grads[0], local_grads[1], local_grads[2], local_grads[3],...  18.4 us
  transfers between devices with their start and end apart: 4, of which 4 were waited for; matrix products, arithmetic and copies ran while one was open for 1% of the time, Pallas kernels for 0%

profile of v1, /device:TPU:0, one launch (start us, length us, event | category | flops | bytes accessed | tf_op | source)
XLA Modules:
  0.0 549.9 jit_solution(15306935509039255713)
XLA Ops:
  7.2 325.0 %while.13 = (s32[]{:T(128)}, f32[16,8,16384]{2,1,0:T(8,128)}, s32[16]{0:T(128)S(1)}, bf16[1,128,8192]{2,1,0:T(8,128)(2,1)}, bf16[1,128,8192]{2,1,0:T(8,128)(2,1)...) while((s32[]{:T(128)}, f32[16,8,16384]{2,1,0:T(8,128)}, s32[16]{0:T(128)S(1)}, ...), condition=%wide.region_1.2_spmd, body=%wide.region_0.1_spmd.sunk | while | flops 2430353408 | bytes 44499364 | solution.py:173
  13.4 1.3 fusion.309
  33.7 1.3 fusion.309
  54.0 1.3 fusion.309
  74.3 1.3 fusion.309
  94.7 1.3 fusion.309
  115.0 1.3 fusion.309
  135.3 1.3 fusion.309
  155.5 1.3 fusion.309
  175.9 1.3 fusion.309
  332.3 7.4 %multiply_bitcast_fusion = f32[128,16384]{1,0:T(8,128)} fusion(f32[16,8,16384]{2,1,0:T(8,128)} %get-tuple-element.175), kind=kLoop, calls=%fused_computation.149 | loop fusion | flops 2097152 | bytes 16777216 | tf_op jit(solution)/shard_map/mul | solution.py:173
  341.9 72.2 %reduce-scatter.2.cloned.1.call-done = f32[128,2048]{1,0:T(8,128)} async-done(((f32[128,16384]{1,0:T(8,128)}), f32[128,2048]{1,0:T(8,128)}) %reduce-scatter.2.cloned.1.call-update) | async-done | bytes 1048592 | tf_op jit(solution)/shard_map/reduce_scatter | solution.py:174
  414.1 2.5 copy.73
  416.6 4.6 all-to-all-start
  423.4 23.4 %all-to-all-done = f32[128,4,512]{0,2,1:T(8,128)S(1)} async-done(((f32[128,4,512]{0,2,1:T(8,128)}), f32[128,4,512]{0,2,1:T(8,128)S(1)}, u32[]{:S(2)}, u32[]{:S(2)}) %all-to-all-start) | async-done | bytes 1048608 | tf_op jit(solution)/shard_map/all_to_all | solution.py:175
  446.8 1.8 multiply_reduce_fusion.1
  450.5 2.2 fusion.118
  452.9 1.7 fusion.113
  454.6 31.0 %all-reduce.9.cloned.1.call-done = f32[512,64]{0,1:T(8,128)} async-done(((f32[512,64]{0,1:T(8,128)}), f32[512,64]{0,1:T(8,128)}) %all-reduce.9.cloned.1.call-update) | async-done | bytes 131088 | tf_op jit(solution)/shard_map/psum | solution.py:182
  485.6 1.3 copy.75
  486.9 18.4 %all-reduce.5 = (f32[64,33]{0,1:T(8,128)S(1)}, f32[64]{0:T(128)S(1)}, f32[64,64]{1,0:T(8,128)S(1)}, f32[2,64]{1,0:T(2,128)S(1)}, f32[512]{0:T(512)S(1)}) all-reduce(f32[64,33]{0,1:T(8,128)S(1)} %fusion.129, f32[64]{0:T(128)S(1)} %get-tuple-element.198, f32[64,64]{1,0:T(8,128)S(1)} %fusion.131, ...), channel_id=1, replica_groups=mesh['dp'=8,'chan'=4] {'chan'}, use_global_device_ids=true, to_apply=%region_3.4 | all-reduce | flops 6912 | bytes 55296 | tf_op jit(solution)/shard_map/psum | solution.py:182
  505.4 23.4 %all-reduce.4 = (f32[64,33]{0,1:T(8,128)}, f32[64]{0:T(128)}, f32[64,64]{1,0:T(8,128)}, f32[2,64]{1,0:T(2,128)}, f32[512]{0:T(512)}) all-reduce(f32[64,33]{0,1:T(8,128)S(1)} %get-tuple-element.214, f32[64]{0:T(128)S(1)} %get-tuple-element.215, f32[64,64]{1,0:T(8,128)S(1)} %get-tuple-element.216, ...), channel_id=1, replica_groups=mesh['dp'=8,'chan'=4] {'dp'}, use_global_device_ids=true, to_apply=%region_4.5 | all-reduce | flops 6912 | bytes 55296 | tf_op jit(solution)/shard_map/psum | solution.py:193
  528.8 13.0 %all-reduce.11.cloned.1.call-done = f32[512,64]{0,1:T(8,128)} async-done(((f32[512,64]{0,1:T(8,128)}), f32[512,64]{0,1:T(8,128)}) %all-reduce.11.cloned.1.call-update) | async-done | bytes 131088 | tf_op jit(solution)/shard_map/psum | solution.py:193
  541.8 1.6 copy.125
  (617 shorter events, 306.0 us)
Async XLA Ops:
  7.2 439.6 %copy-start = (f32[512,64]{0,1:T(8,128)S(1)}, f32[512,64]{0,1:T(8,128)}, u32[]{:S(2)}) copy-start(f32[512,64]{0,1:T(8,128)} %param.16) | copy-start | bytes 393220
  7.2 406.9 %reduce-scatter.2.cloned.1.call-start = ((), (), s32[]{:S(2)}) async-start(), calls=%async_computation.2 | async-start | bytes 9437184 | tf_op jit(solution)/shard_map/reduce_scatter | solution.py:174
  339.7 0.7 copy-start.3
  339.7 82.6 %copy-start.4 = (f32[2,64]{1,0:T(2,128)S(1)}, f32[2,64]{1,0:T(2,128)}, u32[]{:S(2)}) copy-start(f32[2,64]{1,0:T(2,128)} %param.15) | copy-start | bytes 1540
  339.7 82.6 %copy-start.2 = (f32[64,33]{0,1:T(8,128)S(1)}, f32[64,33]{0,1:T(8,128)}, u32[]{:S(2)}) copy-start(f32[64,33]{0,1:T(8,128)} %param.12) | copy-start | bytes 25348
  339.7 82.6 %copy-start.5 = (f32[64]{0:T(128)S(1)}, f32[64]{0:T(128)}, u32[]{:S(2)}) copy-start(f32[64]{0:T(128)} %param.13) | copy-start | bytes 772
  339.7 82.9 %copy-start.1 = (f32[64,64]{1,0:T(8,128)S(1)}, f32[64,64]{1,0:T(8,128)}, u32[]{:S(2)}) copy-start(f32[64,64]{1,0:T(8,128)} %param.14) | copy-start | bytes 49156
  416.6 30.2 %all-to-all-start = ((f32[128,4,512]{0,2,1:T(8,128)}), f32[128,4,512]{0,2,1:T(8,128)S(1)}, u32[]{:S(2)}, u32[]{:S(2)}) async-start(f32[128,4,512]{0,2,1:T(8,128)} %bitcast.39), calls=%async_computation.1 | async-start | bytes 2097152 | tf_op jit(solution)/shard_map/all_to_all | solution.py:175
  421.2 64.4 %all-reduce.9.cloned.1.call-start = ((), (), s32[]{:S(2)}) async-start(), calls=%async_computation.3 | async-start | bytes 262144 | tf_op jit(solution)/shard_map/psum | solution.py:182
  452.7 89.1 %all-reduce.11.cloned.1.call-start = ((), (), s32[]{:S(2)}) async-start(), calls=%async_computation.4 | async-start | bytes 262144 | tf_op jit(solution)/shard_map/psum | solution.py:193
Sparse Core Ops, SparseCore 0:
  339.8 74.2 reduce-scatter.1
  452.8 32.7 all-reduce.8
  488.6 53.0 all-reduce.10
